TPU v7x, 32 devices: a whole 2x2x4 slice. The times are simulated.
32 devices in a mesh: ctx: 16 (over z, x, core), tp: 2 (over y).
Axes of the slice: x: 2, y: 2, z: 4, core: 2. Of those that a mesh axis runs over, the one named last changes fastest.
Arguments:
- doc_lengths: int32 [32], replicated, may hold values from 1 to 512, 2048 in all
- ssm_x: bfloat16 [2048, 8192], P('ctx', 'tp'), may hold values from -6 to 6
- ssm_gate: bfloat16 [2048, 8192], P('ctx', 'tp'), may hold values from -6 to 6
- ssm_b: bfloat16 [2048, 2048], P('ctx', 'tp'), may hold values from -6 to 6
- ssm_c: bfloat16 [2048, 2048], P('ctx', 'tp'), may hold values from -0.375 to 0.375
- step_size: float32 [2048, 128], P('ctx', 'tp'), as said below
- decay_rate: float32 [128], P('tp'), as said below
- norm_weight: float32 [8192], P('tp'), may hold values from 0.1 to 1.9
- queries: bfloat16 [2048, 8192], P('ctx', 'tp'), may hold values from -96 to 96
- keys: bfloat16 [2048, 1024], P('ctx', 'tp'), may hold values from -4 to 4
- values: bfloat16 [2048, 1024], P('ctx', 'tp'), may hold values from -6 to 6
Outputs:
- mixed: bfloat16 [2048, 8192], P(('ctx', 'tp'))
- attended: bfloat16 [2048, 8192], P(('ctx', 'tp'))
Inputs may be any that keep to these rules, and one draw needn't show every extreme that they name: `doc_lengths`: every document has at least one token; the longest has exactly 512. `step_size`: Positive. `decay_rate`: Positive, at most 0.04.
All inputs are finite; a program needn't handle non-finite values.
Results may differ from a plain program's by a relative error of at most 0.0049.
Values may be sent and summed in bfloat16 or wider, within the bound.
A program may use at most 192 MiB of HBM per device.

v0:
```python
import jax
import jax.numpy as jnp
from jax import lax
from jax.sharding import PartitionSpec as P

HEADS = 128
GROUPS = 8
ATT_DIM = 128
DOC_DEVS = 4
NEG_LARGE = -1e30


def for_sending(x):
    return jax.tree.map(lambda a: a.astype(jnp.bfloat16) if a.dtype == jnp.float32 else a, x)


def passed_along(block, axis, distance):
    devices = range(lax.axis_size(axis))
    route = [(i - distance, i) for i in devices if i - distance in devices]
    return lax.ppermute(block, axis, route)


def doc_starts(doc_lengths):
    return jnp.cumsum(doc_lengths) - doc_lengths


def doc_index(positions, starts):
    return jnp.sum((starts[None, :] <= positions[:, None]).astype(jnp.int32), axis=1) - 1


def block_terms(ssm_x, ssm_b, ssm_c, step_size, decay_rate, doc_ids, prev_id, group_heads):
    tok_rows = ssm_x.shape[0]
    head_count = step_size.shape[1]
    group_count = head_count // group_heads
    head_size = ssm_x.shape[1] // head_count
    state_size = ssm_b.shape[1] // group_count
    inputs = ssm_x.reshape(tok_rows, group_count, group_heads, head_size)
    in_proj = ssm_b.reshape(tok_rows, group_count, state_size)
    out_proj = ssm_c.reshape(tok_rows, group_count, state_size)
    log_decay = -(step_size * decay_rate[None, :])
    cumulative = jnp.cumsum(log_decay, axis=0)
    same_doc = doc_ids[:, None] == doc_ids[None, :]
    causal = jnp.arange(tok_rows)[:, None] >= jnp.arange(tok_rows)[None, :]
    allowed = (same_doc & causal)[None]
    spread = cumulative.T[:, :, None] - cumulative.T[:, None, :]
    weights = (
        jnp.where(allowed, jnp.exp(jnp.where(allowed, spread, 0.0)), 0.0) * step_size.T[:, None, :]
    )
    intersection = jnp.einsum("tgn,sgn->gts", out_proj, in_proj, preferred_element_type=jnp.float32)
    mixing = (
        weights.reshape(group_count, group_heads, tok_rows, tok_rows) * intersection[:, None]
    ).astype(jnp.bfloat16)
    y_intra = jnp.einsum("ghts,sghp->tghp", mixing, inputs, preferred_element_type=jnp.float32)
    final_sum = cumulative[-1]
    tail = (
        jnp.exp(final_sum[None, :] - cumulative)
        * step_size
        * (doc_ids == doc_ids[-1]).astype(jnp.float32)[:, None]
    )
    scaled = (
        inputs.astype(jnp.float32) * tail.reshape(tok_rows, group_count, group_heads)[..., None]
    ).astype(jnp.bfloat16)
    state_local = jnp.einsum("sghp,sgn->ghpn", scaled, in_proj, preferred_element_type=jnp.float32)
    entry = jnp.exp(cumulative) * (doc_ids == prev_id).astype(jnp.float32)[:, None]
    transmit = jnp.exp(final_sum) * (doc_ids[-1] == prev_id).astype(jnp.float32)
    return (y_intra, state_local, entry, transmit.reshape(group_count, group_heads))


def finish_rows(y_intra, entry, carried, ssm_c, ssm_gate, norm_weight):
    tok_rows, group_count, group_heads, head_size = y_intra.shape
    out_proj = ssm_c.reshape(tok_rows, group_count, -1).astype(jnp.float32)
    incoming = jnp.einsum("tgn,ghpn->tghp", out_proj, carried, precision=lax.Precision.HIGHEST)
    mixer_out = y_intra + incoming * entry.reshape(tok_rows, group_count, group_heads)[..., None]
    gate_vals = ssm_gate.reshape(tok_rows, group_count, group_heads, head_size).astype(jnp.float32)
    gated = (mixer_out * jax.nn.silu(gate_vals)).reshape(
        tok_rows, group_count, group_heads * head_size
    )
    factor = lax.rsqrt(jnp.mean(gated * gated, axis=2, keepdims=True) + 1e-05)
    return ((gated * factor).reshape(tok_rows, -1) * norm_weight[None, :]).astype(jnp.bfloat16)


def chain_states(earlier, later):
    return (earlier[0] * later[0], later[0][:, :, None, None] * earlier[1] + later[1])


def attention_update(
    carry, query_rows, key_block, value_block, key_pos, query_pos, query_doc, starts
):
    running_max, running_sum, running_acc = carry
    block_rows = key_block.shape[0]
    kv_local = key_block.shape[1] // ATT_DIM
    key_heads = key_block.reshape(block_rows, kv_local, ATT_DIM)
    value_heads = value_block.reshape(block_rows, kv_local, ATT_DIM)
    key_doc = doc_index(key_pos, starts)
    allowed = (query_doc[:, None] == key_doc[None, :]) & (key_pos[None, :] <= query_pos[:, None])
    scores = jnp.einsum(
        "tngd,knd->ngtk", query_rows, key_heads, preferred_element_type=jnp.float32
    ) * ATT_DIM ** (-0.5)
    scores = jnp.where(allowed[None, None], scores, -jnp.inf)
    new_max = jnp.maximum(running_max, jnp.max(scores, axis=3))
    probs = jnp.exp(scores - new_max[..., None])
    factor = jnp.exp(running_max - new_max)
    new_sum = running_sum * factor + jnp.sum(probs, axis=3)
    weighted = jnp.einsum(
        "ngtk,knd->ngtd",
        probs.astype(jnp.bfloat16),
        value_heads,
        preferred_element_type=jnp.float32,
    )
    return (new_max, new_sum, running_acc * factor[..., None] + weighted)


def local(
    doc_lengths,
    ssm_x,
    ssm_gate,
    ssm_b,
    ssm_c,
    step_size,
    decay_rate,
    norm_weight,
    queries,
    keys,
    values,
):
    tok_rows = ssm_x.shape[0]
    ctx_index = lax.axis_index("ctx")
    begin = ctx_index * tok_rows
    positions = begin + jnp.arange(tok_rows, dtype=jnp.int32)
    starts = doc_starts(doc_lengths)
    doc_ids = doc_index(positions, starts)
    prev_id = doc_index(jnp.reshape(begin - 1, (1,)), starts)[0]
    group_heads = HEADS // GROUPS
    y_intra, state_local, entry, transmit = block_terms(
        ssm_x, ssm_b, ssm_c, step_size, decay_rate, doc_ids, prev_id, group_heads
    )
    merged = (transmit, state_local)
    for level_bit in range(DOC_DEVS.bit_length() - 1):
        earlier = passed_along(
            (for_sending(merged[0]), for_sending(merged[1])), "ctx", 1 << level_bit
        )
        merged = chain_states(earlier, merged)
    carried = passed_along(merged[1], "ctx", 1)
    mixed_rows = finish_rows(y_intra, entry, carried, ssm_c, ssm_gate, norm_weight)
    kv_local = keys.shape[1] // ATT_DIM
    q_groups = queries.shape[1] // (kv_local * ATT_DIM)
    query_rows = queries.reshape(tok_rows, kv_local, q_groups, ATT_DIM)
    floor_start = jnp.max(jnp.where(starts <= begin, starts, 0))
    query_last = begin + tok_rows - 1
    carry_shape = (kv_local, q_groups, tok_rows)
    initial = (
        jnp.full(carry_shape, NEG_LARGE, jnp.float32),
        jnp.zeros(carry_shape, jnp.float32),
        jnp.zeros(carry_shape + (ATT_DIM,), jnp.float32),
    )

    def visit(carry, key_block, value_block, key_begin):
        block_rows = key_block.shape[0]
        needed = (key_begin <= query_last) & (key_begin + block_rows - 1 >= floor_start)

        def update(inner):
            key_pos = key_begin + jnp.arange(block_rows, dtype=jnp.int32)
            return attention_update(
                inner, query_rows, key_block, value_block, key_pos, positions, doc_ids, starts
            )

        def unchanged(inner):
            return inner

        return lax.cond(needed, update, unchanged, carry)

    totals = visit(initial, keys, values, begin)
    for hop_count in range(1, DOC_DEVS + 1):
        near_keys, near_values = passed_along((keys, values), "ctx", hop_count)
        totals = visit(totals, near_keys, near_values, begin - hop_count * tok_rows)
    final_out = totals[2] / totals[1][..., None]
    attended_rows = (
        jnp.transpose(final_out, (2, 0, 1, 3)).reshape(tok_rows, -1).astype(jnp.bfloat16)
    )
    mixed_local, attended_local = (
        lax.all_to_all(mixed_rows, "tp", split_axis=0, concat_axis=1, tiled=True),
        lax.all_to_all(attended_rows, "tp", split_axis=0, concat_axis=1, tiled=True),
    )
    return (mixed_local, attended_local)


def solution(mesh):
    return jax.shard_map(
        local,
        mesh=mesh,
        in_specs=(
            P(),
            P("ctx", "tp"),
            P("ctx", "tp"),
            P("ctx", "tp"),
            P("ctx", "tp"),
            P("ctx", "tp"),
            P("tp"),
            P("tp"),
            P("ctx", "tp"),
            P("ctx", "tp"),
            P("ctx", "tp"),
        ),
        out_specs=(P(("ctx", "tp"), None), P(("ctx", "tp"), None)),
        check_vma=False,
    )
```

profile of v0, /device:TPU:26, one launch (start us, length us, event | category | flops | bytes accessed | tf_op | source)
XLA Modules:
  0.0 229.4 jit_solution(9776765901697887157)
XLA Ops:
  0.7 0.8 copy.164
  1.6 1.3 fusion.53
  5.7 0.8 copy.170
  6.6 0.8 multiply_negate_fusion
  8.4 1.6 copy.169
  10.2 3.4 %fusion.61 = (bf16[4,16,64,256]{3,2,1,0:T(8,128)(2,1)}, f32[4,16,64,256]{3,2,1,0:T(8,128)}) fusion(bf16[128,4,256,1]{2,1,0,3:T(4,128)(2,1)S(1)} %bitcast.87, bf16[128,4,16,64]{0,3,2,1:T(8,128)(2,1)S(1)} %bitcast.80, f32[128,4,16]{0,2,1:T(8,128)S(1)} %bitcast.100), kind=kOutput, calls=%fused_computation.124 | convolution fusion | flops 271056896 | bytes 7634944 | tf_op jit(solution)/shard_map/sghp,sgn->ghpn/dot_general | solution.py:63
  13.6 1.9 collective-permute-start.1
  16.2 24.9 %collective-permute-done.1 = bf16[4,16,64,256]{3,2,1,0:T(8,128)(2,1)S(1)} collective-permute-done((bf16[4,16,64,256]{3,2,1,0:T(8,128)(2,1)}, bf16[4,16,64,256]{3,2,1,0:T(8,128)(2,1)S(1)}, u32[]{:S(2)}, u32[]{:S(2)}) %collective-permute-start.1) | collective-permute-done | bytes 2097184 | tf_op jit(solution)/shard_map/ppermute | solution.py:20
  41.1 2.9 %fusion.31 = bf16[4,16,64,256]{3,2,1,0:T(8,128)(2,1)S(1)} fusion(f32[4,16,64,256]{3,2,1,0:T(8,128)} %get-tuple-element.411, bf16[4,16,64,256]{3,2,1,0:T(8,128)(2,1)S(1)} %collective-permute-done.1, f32[4,16]{1,0:T(4,128)S(1)} %mul.225), kind=kLoop, calls=%fused_computation.74 | loop fusion | flops 4194304 | bytes 8388864 | tf_op jit(solution)/shard_map/convert_element_type | solution.py:14
  44.0 1.3 collective-permute-start.2
  45.3 1.9 collective-permute-start
  47.2 41.3 %collective-permute-done = bf16[4,16]{1,0:T(4,128)(2,1)S(1)} collective-permute-done((bf16[4,16]{1,0:T(4,128)(2,1)S(1)}, bf16[4,16]{1,0:T(4,128)(2,1)S(1)}, u32[]{:S(2)}, u32[]{:S(2)}) %collective-permute-start) | collective-permute-done | bytes 160 | tf_op jit(solution)/shard_map/ppermute | solution.py:20
  88.6 2.9 %collective-permute-done.2 = bf16[4,16,64,256]{3,2,1,0:T(8,128)(2,1)S(1)} collective-permute-done((bf16[4,16,64,256]{3,2,1,0:T(8,128)(2,1)S(1)}, bf16[4,16,64,256]{3,2,1,0:T(8,128)(2,1)S(1)}, u32[]{:S(2)}, u32[]{:S(2)}) %collective-permute-start.2) | collective-permute-done | bytes 2097184 | tf_op jit(solution)/shard_map/ppermute | solution.py:20
  91.5 2.8 %multiply_add_fusion.8 = f32[4,16,64,256]{3,2,1,0:T(8,128)} fusion(bf16[4,16,64,256]{3,2,1,0:T(8,128)(2,1)S(1)} %collective-permute-done.2, f32[4,16,64,256]{3,2,1,0:T(8,128)S(1)} %copy-done, bf16[4,16,64,256]{3,2,1,0:T(8,128)(2,1)S(1)} %collective-permute-done.1, f32[4,16]{1,0:T(4,128)S(1)} %mul.225, f32[4,16]{1,0:T(4,128)S(1)} %convert_multiply_fusion), kind=kLoop, calls=%fused_computation.71 | loop fusion | flops 6291456 | bytes 12583424 | tf_op jit(solution)/shard_map/add | solution.py:83
  94.3 1.9 collective-permute-start.3
  96.2 1.9 collective-permute-start.4
  98.2 1.3 collective-permute-start.6
  99.5 1.9 collective-permute-start.5
  101.4 1.3 collective-permute-start.7
  102.9 1.2 fusion.44
  104.1 4.2 %fusion.32 = f32[4,16,128,64]{2,3,1,0:T(8,128)} fusion(bf16[128,4,16,64]{0,3,2,1:T(8,128)(2,1)S(1)} %bitcast.81, f32[4,128,128]{2,1,0:T(8,128)S(1)} %fusion.44, f32[4,16,128]{2,1,0:T(8,128)} %bitcast.101, f32[4,16,128]{2,1,0:T(8,128)S(1)} %bitcast.103, pred[128,128]{1,0:T(8,128)(4,1)S(1)} %fusion.51), kind=kOutput, calls=%fused_computation.75 | convolution fusion | flops 140509184 | bytes 3489792 | tf_op jit(solution)/shard_map/ghts,sghp->tghp/dot_general | solution.py:53
  109.7 0.9 reshape.555
  110.6 1.6 copy.179
  114.2 1.6 copy.175
  115.8 7.4 %conditional.5 = (f32[4,8,128]{2,1,0:T(8,128)}, f32[4,8,128]{2,1,0:T(8,128)S(1)}, f32[4,8,128,128]{3,2,1,0:T(8,128)S(1)}) conditional(s32[]{:T(128)} %convert_element_type.138, () %tuple.41, (s32[128]{0:T(128)S(1)}, s32[32]{0:T(128)S(1)}, s32[]{:T(128)}, s32[128]{0:T(128)S(1)}, bf16[128,512]{1,0:T(8,128)(2,1)}, ...), branch_computations={%region_6.7_spmd, %region_7.11_spmd} | conditional | flops 272707712 | bytes 18830008 | solution.py:170
  116.0 0.9 reshape.536
  118.1 1.1 fusion.1
  119.9 0.9 reshape.537
  120.9 2.3 %convolution_add_fusion = f32[4,8,128,128]{3,2,1,0:T(8,128)S(1)} fusion(f32[4,8,128,128]{2,3,1,0:T(8,128)} %copy-done.5, f32[4,8,128]{2,1,0:T(8,128)S(1)} %get-tuple-element.383, f32[4,8,128]{2,1,0:T(8,128)} %get-tuple-element.417, bf16[128,4,128,1]{2,1,0,3:T(4,128)(2,1)S(1)} %bitcast.98), kind=kOutput, calls=%fused_computation.4 | convolution fusion | flops 135790592 | bytes 4358144 | tf_op jit(solution)/shard_map/cond/branch_1_fun/ngtk,knd->ngtd/dot_general | solution.py:104
  123.2 25.5 %collective-permute-done.4 = bf16[128,512]{1,0:T(8,128)(2,1)} collective-permute-done((bf16[128,512]{1,0:T(8,128)(2,1)}, bf16[128,512]{1,0:T(8,128)(2,1)}, u32[]{:S(2)}, u32[]{:S(2)}) %collective-permute-start.4) | collective-permute-done | bytes 131104 | tf_op jit(solution)/shard_map/ppermute | solution.py:20
  148.7 1.3 collective-permute-start.8
  150.0 1.5 collective-permute-done.5
  151.5 1.3 collective-permute-start.9
  152.8 1.3 collective-permute-start.10
  154.1 1.3 collective-permute-start.11
  155.4 8.1 %conditional.6 = ((f32[4,8,128]{2,1,0:T(8,128)}, f32[4,8,128]{2,1,0:T(8,128)S(1)}, f32[4,8,128,128]{3,2,1,0:T(8,128)S(1)})) conditional(s32[]{:T(128)} %convert_element_type.137, (f32[4,8,128]{2,1,0:T(8,128)}, f32[4,8,128]{2,1,0:T(8,128)S(1)}, f32[4,8,128,128]{3,2,1,0:T(8,128)S(1)}) %conditional.5, (s32[128]{0:T(128)S(1)}, s32[32]{0:T(128)S(1)}, ...), branch_computations={%region_11.12_spmd, %region_12.16_spmd} | conditional | flops 273223808 | bytes 21009088 | solution.py:170
  155.6 0.9 reshape.538
  159.5 0.9 reshape.539
  160.5 2.4 %multiply_add_fusion = f32[4,8,128,128]{3,2,1,0:T(8,128)S(1)} fusion(f32[4,8,128,128]{3,2,1,0:T(8,128)S(1)} %get-tuple-element.131, f32[4,8,128,128]{2,3,1,0:T(8,128)} %copy-done.1, f32[4,8,128]{2,1,0:T(8,128)S(1)} %get-tuple-element.386, f32[4,8,128]{2,1,0:T(8,128)S(1)} %max.8, bf16[128,4,128,1]{2,1,0,3:T(4,128)(2,1)S(1)} %bitcast.92), kind=kOutput, calls=%fused_computation.16 | convolution fusion | flops 136314880 | bytes 6455296 | tf_op jit(solution)/shard_map/cond/branch_1_fun/ngtk,knd->ngtd/dot_general | solution.py:104
  163.5 8.0 %conditional.7 = ((f32[4,8,128]{2,1,0:T(8,128)}, f32[4,8,128]{2,1,0:T(8,128)S(1)}, f32[4,8,128,128]{3,2,1,0:T(8,128)S(1)})) conditional(s32[]{:T(128)} %convert_element_type.136, (f32[4,8,128]{2,1,0:T(8,128)}, f32[4,8,128]{2,1,0:T(8,128)S(1)}, f32[4,8,128,128]{3,2,1,0:T(8,128)S(1)}) %get-tuple-element.442, (s32[128]{0:T(128)S(1)}, ...), branch_computations={%region_16.17_spmd, %region_17.21_spmd} | conditional | flops 273223808 | bytes 21009088 | solution.py:170
  163.7 0.9 reshape.540
  167.5 0.9 reshape.541
  168.5 2.4 %multiply_add_fusion.2 = f32[4,8,128,128]{3,2,1,0:T(8,128)S(1)} fusion(f32[4,8,128,128]{3,2,1,0:T(8,128)S(1)} %get-tuple-element.141, f32[4,8,128,128]{2,3,1,0:T(8,128)} %copy-done.2, f32[4,8,128]{2,1,0:T(8,128)S(1)} %get-tuple-element.388, f32[4,8,128]{2,1,0:T(8,128)S(1)} %max.9, bf16[128,4,128,1]{2,1,0,3:T(4,128)(2,1)S(1)} %bitcast.94), kind=kOutput, calls=%fused_computation.30 | convolution fusion | flops 136314880 | bytes 6455296 | tf_op jit(solution)/shard_map/cond/branch_1_fun/ngtk,knd->ngtd/dot_general | solution.py:104
  171.5 8.0 %conditional.8 = ((f32[4,8,128]{2,1,0:T(8,128)}, f32[4,8,128]{2,1,0:T(8,128)S(1)}, f32[4,8,128,128]{3,2,1,0:T(8,128)S(1)})) conditional(s32[]{:T(128)} %convert_element_type.135, (f32[4,8,128]{2,1,0:T(8,128)}, f32[4,8,128]{2,1,0:T(8,128)S(1)}, f32[4,8,128,128]{3,2,1,0:T(8,128)S(1)}) %get-tuple-element.443, (s32[128]{0:T(128)S(1)}, ...), branch_computations={%region_21.22_spmd, %region_22.26_spmd} | conditional | flops 273223808 | bytes 21009088 | solution.py:170
  171.7 0.9 reshape.542
  173.1 0.7 max.10
  175.6 0.9 reshape.543
  176.5 2.4 %multiply_add_fusion.4 = f32[4,8,128,128]{3,2,1,0:T(8,128)S(1)} fusion(f32[4,8,128,128]{3,2,1,0:T(8,128)S(1)} %get-tuple-element.151, f32[4,8,128,128]{2,3,1,0:T(8,128)} %copy-done.3, f32[4,8,128]{2,1,0:T(8,128)S(1)} %get-tuple-element.390, f32[4,8,128]{2,1,0:T(8,128)S(1)} %max.10, bf16[128,4,128,1]{2,1,0,3:T(4,128)(2,1)S(1)} %bitcast.96), kind=kOutput, calls=%fused_computation.44 | convolution fusion | flops 136314880 | bytes 6455296 | tf_op jit(solution)/shard_map/cond/branch_1_fun/ngtk,knd->ngtd/dot_general | solution.py:104
  179.5 6.5 %conditional.9 = ((f32[4,8,128]{2,1,0:T(8,128)S(1)}, f32[4,8,128,128]{3,2,1,0:T(8,128)S(1)})) conditional(s32[]{:T(128)} %convert_element_type.134, (f32[4,8,128]{2,1,0:T(8,128)S(1)}, f32[4,8,128,128]{3,2,1,0:T(8,128)S(1)}) %tuple.46, (s32[128]{0:T(128)S(1)}, s32[32]{0:T(128)S(1)}, s32[]{:T(128)}, s32[128]{0:T(128)S(1)}, ...), branch_computations={%region_26.27_spmd, %region_27.31_spmd} | conditional | flops 273223808 | bytes 20976312 | solution.py:170
  180.2 0.7 max.11
  182.7 0.9 reshape.545
  183.7 2.4 %multiply_add_fusion.6 = f32[4,8,128,128]{3,2,1,0:T(8,128)S(1)} fusion(f32[4,8,128,128]{3,2,1,0:T(8,128)S(1)} %get-tuple-element.161, f32[4,8,128,128]{2,3,1,0:T(8,128)} %copy-done.4, f32[4,8,128]{2,1,0:T(8,128)S(1)} %get-tuple-element.392, f32[4,8,128]{2,1,0:T(8,128)S(1)} %max.11, bf16[128,4,128,1]{2,1,0,3:T(4,128)(2,1)S(1)} %bitcast.89), kind=kOutput, calls=%fused_computation.58 | convolution fusion | flops 136314880 | bytes 6455296 | tf_op jit(solution)/shard_map/cond/branch_1_fun/ngtk,knd->ngtd/dot_general | solution.py:104
  187.5 1.3 convert_element_type.141
  188.8 3.6 %all-to-all-start.1 = ((bf16[2,64,4096]{2,1,0:T(8,128)(2,1)}), bf16[2,64,4096]{2,1,0:T(8,128)(2,1)S(1)}, u32[]{:S(2)}, u32[]{:S(2)}) async-start(bf16[2,64,4096]{2,1,0:T(8,128)(2,1)} %convert_element_type.141), calls=%async_computation.1 | async-start | bytes 2097152 | tf_op jit(solution)/shard_map/all_to_all | solution.py:182
  192.4 5.8 %multiply_reduce_fusion = (f32[128,4]{0,1:T(4,128)S(1)}, f32[128,4,16,64]{0,3,2,1:T(8,128)S(1)}) fusion(f32[128,4,16,64]{0,3,2,1:T(8,128)} %bitcast.82, f32[128,4,16]{0,2,1:T(8,128)S(1)} %broadcast_multiply_fusion, f32[4,16,64,256]{3,2,1,0:T(8,128)} %collective-permute-done.3, bf16[128,4,256,1]{2,1,0,3:T(4,128)(2,1)S(1)} %bitcast.99, ...), kind=kOutput, calls=%fused_computation.81 | convolution fusion | flops 1615330816 | bytes 10782720 | tf_op jit(solution)/shard_map/tgn,ghpn->tghp/dot_general | solution.py:72
  198.1 3.7 %reshape.573 = f32[2,64,4096]{1,0,2:T(2,128)} reshape(f32[128,4,16,64]{0,3,2,1:T(8,128)S(1)} %get-tuple-element.413) | data formatting | bytes 4194304 | tf_op jit(solution)/shard_map/reshape | solution.py:75
  201.8 5.3 %copy.233 = f32[2,64,4096]{2,1,0:T(8,128)S(1)} copy(f32[2,64,4096]{1,0,2:T(2,128)} %reshape.573) | data formatting | bytes 4194304 | tf_op jit(solution)/shard_map/reshape | solution.py:75
  207.2 1.7 mul.244
  208.9 3.7 %mul.245 = f32[2,64,4096]{2,1,0:T(8,128)} reshape(f32[128,4,1024]{2,1,0:T(4,128)} %mul.244) | data formatting | bytes 4194304 | tf_op jit(solution)/shard_map/mul | solution.py:79
  212.6 2.8 %multiply_convert_fusion.2 = bf16[2,64,4096]{2,1,0:T(8,128)(2,1)} fusion(f32[2,64,4096]{2,1,0:T(8,128)S(1)} %copy.233, f32[2,64,4096]{2,1,0:T(8,128)} %mul.245, f32[4096]{0:T(1024)S(1)} %copy-done.10), kind=kLoop, calls=%fused_computation.80 | loop fusion | flops 1572864 | bytes 5259264 | tf_op jit(solution)/shard_map/convert_element_type | solution.py:79
  215.4 3.6 %all-to-all-start = ((bf16[2,64,4096]{2,1,0:T(8,128)(2,1)}), bf16[2,64,4096]{2,1,0:T(8,128)(2,1)S(1)}, u32[]{:S(2)}, u32[]{:S(2)}) async-start(bf16[2,64,4096]{2,1,0:T(8,128)(2,1)} %multiply_convert_fusion.2), calls=%async_computation | async-start | bytes 2097152 | tf_op jit(solution)/shard_map/all_to_all | solution.py:181
  219.0 1.1 copy.237
  220.1 8.3 %all-to-all-done = bf16[2,64,4096]{2,1,0:T(8,128)(2,1)S(1)} async-done(((bf16[2,64,4096]{2,1,0:T(8,128)(2,1)}), bf16[2,64,4096]{2,1,0:T(8,128)(2,1)S(1)}, u32[]{:S(2)}, u32[]{:S(2)}) %all-to-all-start) | async-done | bytes 1048608 | tf_op jit(solution)/shard_map/all_to_all | solution.py:181
  228.4 1.1 copy.236
  (99 shorter events, 20.2 us)
Async XLA Ops:
  0.6 9.4 %copy-start.7 = (bf16[128,1024]{1,0:T(8,128)(2,1)S(1)}, bf16[128,1024]{1,0:T(8,128)(2,1)}, u32[]{:S(2)}) copy-start(bf16[128,1024]{1,0:T(8,128)(2,1)} %param.24) | copy-start | bytes 786436
  2.9 4.5 %copy-start.11 = (s32[32]{0:T(128)}, s32[32]{0:T(128)S(1)}, u32[]{:S(2)}) copy-start(s32[32]{0:T(128)S(1)} %get-tuple-element.393) | copy-start | bytes 388
  13.6 27.6 %collective-permute-start.1 = (bf16[4,16,64,256]{3,2,1,0:T(8,128)(2,1)}, bf16[4,16,64,256]{3,2,1,0:T(8,128)(2,1)S(1)}, u32[]{:S(2)}, u32[]{:S(2)}) collective-permute-start(bf16[4,16,64,256]{3,2,1,0:T(8,128)(2,1)} %get-tuple-element.410), channel_id=1, source_target_pairs={{0,2},{2,4},{4,6},{6,8},{8,10},{10,12},{12,14},{14,16},{16,18},{18... | collective-permute-start | bytes 6291464 | tf_op jit(solution)/shard_map/ppermute | solution.py:20
  41.1 50.4 %copy-start = (f32[4,16,64,256]{3,2,1,0:T(8,128)S(1)}, f32[4,16,64,256]{3,2,1,0:T(8,128)}, u32[]{:S(2)}) copy-start(f32[4,16,64,256]{3,2,1,0:T(8,128)} %get-tuple-element.411) | copy-start | bytes 12582916
  44.0 47.5 %collective-permute-start.2 = (bf16[4,16,64,256]{3,2,1,0:T(8,128)(2,1)S(1)}, bf16[4,16,64,256]{3,2,1,0:T(8,128)(2,1)S(1)}, u32[]{:S(2)}, u32[]{:S(2)}) collective-permute-start(bf16[4,16,64,256]{3,2,1,0:T(8,128)(2,1)S(1)} %fusion.31), channel_id=1, source_target_pairs={{0,4},{2,6},{4,8},{6,10},{8,12},{10,14},{12,16},{14,18},{16,20},{1... | collective-permute-start | bytes 6291464 | tf_op jit(solution)/shard_map/ppermute | solution.py:20
  45.3 43.2 %collective-permute-start = (bf16[4,16]{1,0:T(4,128)(2,1)S(1)}, bf16[4,16]{1,0:T(4,128)(2,1)S(1)}, u32[]{:S(2)}, u32[]{:S(2)}) collective-permute-start(bf16[4,16]{1,0:T(4,128)(2,1)S(1)} %convert_element_type.121), channel_id=1, source_target_pairs={{0,2},{2,4},{4,6},{6,8},{8,10},{10,12},{12,14},{14,16},{16,18},{18... | collective-permute-start | bytes 392 | tf_op jit(solution)/shard_map/ppermute | solution.py:20
  94.3 98.0 %collective-permute-start.3 = (f32[4,16,64,256]{3,2,1,0:T(8,128)}, f32[4,16,64,256]{3,2,1,0:T(8,128)}, u32[]{:S(2)}, u32[]{:S(2)}) collective-permute-start(f32[4,16,64,256]{3,2,1,0:T(8,128)} %multiply_add_fusion.8), channel_id=1, source_target_pairs={{0,2},{2,4},{4,6},{6,8},{8,10},{10,12},{12,14},{14,16},{16,18},{18... | collective-permute-start | bytes 12582920 | tf_op jit(solution)/shard_map/ppermute | solution.py:20
  96.2 52.4 %collective-permute-start.4 = (bf16[128,512]{1,0:T(8,128)(2,1)}, bf16[128,512]{1,0:T(8,128)(2,1)}, u32[]{:S(2)}, u32[]{:S(2)}) collective-permute-start(bf16[128,512]{1,0:T(8,128)(2,1)} %param.30), channel_id=1, source_target_pairs={{0,2},{2,4},{4,6},{6,8},{8,10},{10,12},{12,14},{14,16},{16,18},{18... | collective-permute-start | bytes 393224 | tf_op jit(solution)/shard_map/ppermute | solution.py:20
  98.2 54.6 %collective-permute-start.6 = (bf16[128,512]{1,0:T(8,128)(2,1)}, bf16[128,512]{1,0:T(8,128)(2,1)}, u32[]{:S(2)}, u32[]{:S(2)}) collective-permute-start(bf16[128,512]{1,0:T(8,128)(2,1)} %param.30), channel_id=1, source_target_pairs={{0,4},{2,6},{4,8},{6,10},{8,12},{10,14},{12,16},{14,18},{16,20},{1... | collective-permute-start | bytes 393224 | tf_op jit(solution)/shard_map/ppermute | solution.py:20
  99.5 52.0 %collective-permute-start.5 = (bf16[128,512]{1,0:T(8,128)(2,1)}, bf16[128,512]{1,0:T(8,128)(2,1)}, u32[]{:S(2)}, u32[]{:S(2)}) collective-permute-start(bf16[128,512]{1,0:T(8,128)(2,1)} %param.31), channel_id=1, source_target_pairs={{0,2},{2,4},{4,6},{6,8},{8,10},{10,12},{12,14},{14,16},{16,18},{18... | collective-permute-start | bytes 393224 | tf_op jit(solution)/shard_map/ppermute | solution.py:20
  101.4 52.7 %collective-permute-start.7 = (bf16[128,512]{1,0:T(8,128)(2,1)}, bf16[128,512]{1,0:T(8,128)(2,1)}, u32[]{:S(2)}, u32[]{:S(2)}) collective-permute-start(bf16[128,512]{1,0:T(8,128)(2,1)} %param.31), channel_id=1, source_target_pairs={{0,4},{2,6},{4,8},{6,10},{8,12},{10,14},{12,16},{14,18},{16,20},{1... | collective-permute-start | bytes 393224 | tf_op jit(solution)/shard_map/ppermute | solution.py:20
  104.1 5.6 %copy-start.8 = (bf16[128,1024]{1,0:T(8,128)(2,1)S(1)}, bf16[128,1024]{1,0:T(8,128)(2,1)}, u32[]{:S(2)}) copy-start(bf16[128,1024]{1,0:T(8,128)(2,1)} %param.25) | copy-start | bytes 786436
  108.3 6.0 %copy-start.6 = (bf16[128,4096]{1,0:T(8,128)(2,1)S(1)}, bf16[128,4096]{1,0:T(8,128)(2,1)}, u32[]{:S(2)}) copy-start(bf16[128,4096]{1,0:T(8,128)(2,1)} %param.23) | copy-start | bytes 3145732
  108.3 6.0 %copy-start.12 = (s32[32]{0:T(128)S(1)}, s32[32]{0:T(128)}, u32[]{:S(2)}) copy-start(s32[32]{0:T(128)} %copy-done.11) | copy-start | bytes 388
  117.4 3.5 %copy-start.5 = (f32[4,8,128,128]{2,3,1,0:T(8,128)}, f32[4,8,128,128]{2,3,1,0:T(8,128)S(1)}, u32[]{:S(2)}) copy-start(f32[4,8,128,128]{2,3,1,0:T(8,128)S(1)} %get-tuple-element.395) | copy-start | bytes 6291460 | tf_op jit(solution)/shard_map/cond
  148.7 22.8 %collective-permute-start.8 = (bf16[128,512]{1,0:T(8,128)(2,1)}, bf16[128,512]{1,0:T(8,128)(2,1)}, u32[]{:S(2)}, u32[]{:S(2)}) collective-permute-start(bf16[128,512]{1,0:T(8,128)(2,1)} %param.30), channel_id=1, source_target_pairs={{0,6},{2,8},{4,10},{6,12},{8,14},{10,16},{12,18},{14,20},{16,22},{... | collective-permute-start | bytes 393224 | tf_op jit(solution)/shard_map/ppermute | solution.py:20
  151.5 20.0 %collective-permute-start.9 = (bf16[128,512]{1,0:T(8,128)(2,1)}, bf16[128,512]{1,0:T(8,128)(2,1)}, u32[]{:S(2)}, u32[]{:S(2)}) collective-permute-start(bf16[128,512]{1,0:T(8,128)(2,1)} %param.31), channel_id=1, source_target_pairs={{0,6},{2,8},{4,10},{6,12},{8,14},{10,16},{12,18},{14,20},{16,22},{... | collective-permute-start | bytes 393224 | tf_op jit(solution)/shard_map/ppermute | solution.py:20
  152.8 26.7 %collective-permute-start.10 = (bf16[128,512]{1,0:T(8,128)(2,1)}, bf16[128,512]{1,0:T(8,128)(2,1)S(1)}, u32[]{:S(2)}, u32[]{:S(2)}) collective-permute-start(bf16[128,512]{1,0:T(8,128)(2,1)} %param.30), channel_id=1, source_target_pairs={{0,8},{2,10},{4,12},{6,14},{8,16},{10,18},{12,20},{14,22},{16,24},... | collective-permute-start | bytes 393224 | tf_op jit(solution)/shard_map/ppermute | solution.py:20
  154.1 25.4 %collective-permute-start.11 = (bf16[128,512]{1,0:T(8,128)(2,1)}, bf16[128,512]{1,0:T(8,128)(2,1)}, u32[]{:S(2)}, u32[]{:S(2)}) collective-permute-start(bf16[128,512]{1,0:T(8,128)(2,1)} %param.31), channel_id=1, source_target_pairs={{0,8},{2,10},{4,12},{6,14},{8,16},{10,18},{12,20},{14,22},{16,24},... | collective-permute-start | bytes 393224 | tf_op jit(solution)/shard_map/ppermute | solution.py:20
  157.0 1.4 copy-start.1
  165.0 1.4 copy-start.2
  173.1 1.4 copy-start.3
  180.2 1.4 copy-start.4
  187.5 4.9 %copy-start.9 = (bf16[128,4,256]{2,1,0:T(4,128)(2,1)S(1)}, bf16[128,4,256]{2,1,0:T(4,128)(2,1)}, u32[]{:S(2)}) copy-start(bf16[128,4,256]{2,1,0:T(4,128)(2,1)} %reshape.555) | copy-start | bytes 786436
  188.8 26.7 %all-to-all-start.1 = ((bf16[2,64,4096]{2,1,0:T(8,128)(2,1)}), bf16[2,64,4096]{2,1,0:T(8,128)(2,1)S(1)}, u32[]{:S(2)}, u32[]{:S(2)}) async-start(bf16[2,64,4096]{2,1,0:T(8,128)(2,1)} %convert_element_type.141), calls=%async_computation.1 | async-start | bytes 2097152 | tf_op jit(solution)/shard_map/all_to_all | solution.py:182
  208.9 3.7 %copy-start.10 = (f32[4096]{0:T(1024)S(1)}, f32[4096]{0:T(1024)}, u32[]{:S(2)}) copy-start(f32[4096]{0:T(1024)} %param.28) | copy-start | bytes 49156
  215.4 13.0 %all-to-all-start = ((bf16[2,64,4096]{2,1,0:T(8,128)(2,1)}), bf16[2,64,4096]{2,1,0:T(8,128)(2,1)S(1)}, u32[]{:S(2)}, u32[]{:S(2)}) async-start(bf16[2,64,4096]{2,1,0:T(8,128)(2,1)} %multiply_convert_fusion.2), calls=%async_computation | async-start | bytes 2097152 | tf_op jit(solution)/shard_map/all_to_all | solution.py:181
where the time goes:
time: 231 us; the launch traced here: 229 us
  waiting for transfers between devices  104 us (45%)
  local copies, waits for them, and re-layouts  40.5 us (18%)
  matrix products  28.5 us (12%)
  starting transfers between devices  25.8 us (11%)
  other arithmetic  24.3 us (11%)
  between operations  5.7 us (2%)
    ppermute x12, waiting for transfers between devices, passed_along(): return lax.ppermute(block, axis, route)  96.1 us
    ppermute x12, starting transfers between devices, passed_along(): return lax.ppermute(block, axis, route)  18.6 us
    dot_general x5, matrix products, attention_update(): jnp.einsum('ngtk,knd->ngtd', probs.astype(jnp.bfloat16), value_heads, pre...  11.8 us
    reshape x2, local copies, waits for them, and re-layouts, finish_rows(): (mixer_out * jax.nn.silu(gate_vals)).reshape(tok_rows, group_count, group...  8.96 us
    all_to_all x1, waiting for transfers between devices, local(): lax.all_to_all(mixed_rows, 'tp', split_axis=0, concat_axis=1, tiled=True)  8.3 us
    dot_general x1, matrix products, finish_rows(): jnp.einsum('tgn,ghpn->tghp', out_proj, carried, precision=lax.Precision.H...  5.78 us
    mul x2, local copies, waits for them, and re-layouts, finish_rows(): gated * factor  5.36 us
    reshape x5, local copies, waits for them, and re-layouts, attention_update(): value_heads = value_block.reshape(block_rows, kv_local, ATT_DIM)  4.7 us
  transfers between devices with their start and end apart: 14, of which 6 were waited for; matrix products, arithmetic and copies ran while one was open for 32% of the time, Pallas kernels for 0%

commit v1 on v0

--- a/solution.py
+++ b/solution.py
@@ -178,7 +178,12 @@
         jnp.transpose(final_out, (2, 0, 1, 3)).reshape(tok_rows, -1).astype(jnp.bfloat16)
     )
     mixed_local, attended_local = (
-        lax.all_to_all(mixed_rows, "tp", split_axis=0, concat_axis=1, tiled=True),
+        jnp.concatenate(
+            lax.all_to_all(
+                jnp.stack(jnp.split(mixed_rows, lax.axis_size("tp"), axis=0)), "tp", 0, 0
+            ),
+            axis=1,
+        ),
         lax.all_to_all(attended_rows, "tp", split_axis=0, concat_axis=1, tiled=True),
     )
     return (mixed_local, attended_local)

time: 231 us -> 223 us (0.965)
  local copies, waits for them, and re-layouts: 40.5 us -> 31.8 us
    reshape x2 -> x1, local copies, waits for them, and re-layouts: 8.96 us -> 2.92 us  [finish_rows(): (mixer_out * jax.nn.silu(gate_vals)).reshape(tok_rows, group_count, group...]
    mul x2 -> x1, local copies, waits for them, and re-layouts: 5.36 us -> 0.34 us  [finish_rows(): gated * factor]
    unnamed x19 -> x22, local copies, waits for them, and re-layouts: 4.14 us -> 5.79 us
  transfers between devices with their start and end apart: 14 -> 14, of which waited for: 6 -> 6; matrix products, arithmetic and copies ran while one was open for 32% -> 29% of each run, Pallas kernels for 0% -> 0%
where the time goes in v1:
time: 223 us; the launch traced here: 221 us
  waiting for transfers between devices  104 us (47%)
  local copies, waits for them, and re-layouts  31.8 us (14%)
  matrix products  29.3 us (13%)
  starting transfers between devices  25.9 us (12%)
  other arithmetic  24.4 us (11%)
  between operations  5.73 us (3%)
    ppermute x12, waiting for transfers between devices, passed_along(): return lax.ppermute(block, axis, route)  95.4 us
    ppermute x12, starting transfers between devices, passed_along(): return lax.ppermute(block, axis, route)  18.6 us
    dot_general x5, matrix products, attention_update(): jnp.einsum('ngtk,knd->ngtd', probs.astype(jnp.bfloat16), value_heads, pre...  11.8 us
    all_to_all x1, waiting for transfers between devices, local(): lax.all_to_all(jnp.stack(jnp.split(mixed_rows, lax.axis_size('tp'), axis=...  8.33 us
    dot_general x1, matrix products, finish_rows(): jnp.einsum('tgn,ghpn->tghp', out_proj, carried, precision=lax.Precision.H...  6.59 us
    unnamed x22, local copies, waits for them, and re-layouts  5.79 us
    cond x13, local copies, waits for them, and re-layouts  4.93 us
    reshape x5, local copies, waits for them, and re-layouts, attention_update(): value_heads = value_block.reshape(block_rows, kv_local, ATT_DIM)  4.7 us
  transfers between devices with their start and end apart: 14, of which 6 were waited for; matrix products, arithmetic and copies ran while one was open for 29% of the time, Pallas kernels for 0%

profile of v1, /device:TPU:26, one launch (start us, length us, event | category | flops | bytes accessed | tf_op | source)
XLA Modules:
  0.0 221.2 jit_solution(10508418064444422161)
XLA Ops:
  0.7 0.8 copy.236
  1.6 1.3 fusion.53
  5.7 0.8 copy.242
  6.6 0.8 multiply_negate_fusion
  8.4 1.6 copy.241
  10.2 3.4 %fusion.61 = (bf16[4,16,64,256]{3,2,1,0:T(8,128)(2,1)}, f32[4,16,64,256]{3,2,1,0:T(8,128)}) fusion(bf16[128,4,256,1]{2,1,0,3:T(4,128)(2,1)S(1)} %bitcast.93, bf16[128,4,16,64]{0,3,2,1:T(8,128)(2,1)S(1)} %bitcast.85, f32[128,4,16]{0,2,1:T(8,128)S(1)} %bitcast.106), kind=kOutput, calls=%fused_computation.127 | convolution fusion | flops 271056896 | bytes 7634944 | tf_op jit(solution)/shard_map/sghp,sgn->ghpn/dot_general | solution.py:63
  13.6 1.9 collective-permute-start.1
  16.2 24.9 %collective-permute-done.1 = bf16[4,16,64,256]{3,2,1,0:T(8,128)(2,1)S(1)} collective-permute-done((bf16[4,16,64,256]{3,2,1,0:T(8,128)(2,1)}, bf16[4,16,64,256]{3,2,1,0:T(8,128)(2,1)S(1)}, u32[]{:S(2)}, u32[]{:S(2)}) %collective-permute-start.1) | collective-permute-done | bytes 2097184 | tf_op jit(solution)/shard_map/ppermute | solution.py:20
  41.1 2.9 %fusion.31 = bf16[4,16,64,256]{3,2,1,0:T(8,128)(2,1)S(1)} fusion(f32[4,16,64,256]{3,2,1,0:T(8,128)} %get-tuple-element.507, bf16[4,16,64,256]{3,2,1,0:T(8,128)(2,1)S(1)} %collective-permute-done.1, f32[4,16]{1,0:T(4,128)S(1)} %mul.223), kind=kLoop, calls=%fused_computation.74 | loop fusion | flops 4194304 | bytes 8388864 | tf_op jit(solution)/shard_map/convert_element_type | solution.py:14
  44.0 1.3 collective-permute-start.2
  45.3 1.9 collective-permute-start
  47.2 41.3 %collective-permute-done = bf16[4,16]{1,0:T(4,128)(2,1)S(1)} collective-permute-done((bf16[4,16]{1,0:T(4,128)(2,1)S(1)}, bf16[4,16]{1,0:T(4,128)(2,1)S(1)}, u32[]{:S(2)}, u32[]{:S(2)}) %collective-permute-start) | collective-permute-done | bytes 160 | tf_op jit(solution)/shard_map/ppermute | solution.py:20
  88.6 2.9 %collective-permute-done.2 = bf16[4,16,64,256]{3,2,1,0:T(8,128)(2,1)S(1)} collective-permute-done((bf16[4,16,64,256]{3,2,1,0:T(8,128)(2,1)S(1)}, bf16[4,16,64,256]{3,2,1,0:T(8,128)(2,1)S(1)}, u32[]{:S(2)}, u32[]{:S(2)}) %collective-permute-start.2) | collective-permute-done | bytes 2097184 | tf_op jit(solution)/shard_map/ppermute | solution.py:20
  91.5 2.9 %multiply_add_fusion.8 = f32[4,16,64,256]{3,2,1,0:T(8,128)} fusion(bf16[4,16,64,256]{3,2,1,0:T(8,128)(2,1)S(1)} %collective-permute-done.2, f32[4,16,64,256]{3,2,1,0:T(8,128)S(1)} %copy-done, bf16[4,16,64,256]{3,2,1,0:T(8,128)(2,1)S(1)} %collective-permute-done.1, f32[4,16]{1,0:T(4,128)S(1)} %mul.223, f32[4,16]{1,0:T(4,128)S(1)} %convert_multiply_fusion), kind=kLoop, calls=%fused_computation.71 | loop fusion | flops 6291456 | bytes 12583424 | tf_op jit(solution)/shard_map/add | solution.py:83
  94.4 1.9 collective-permute-start.3
  96.3 1.9 collective-permute-start.4
  98.2 1.3 collective-permute-start.6
  99.5 1.9 collective-permute-start.5
  101.5 1.3 collective-permute-start.7
  102.9 1.2 fusion.44
  104.1 4.2 %fusion.32 = f32[4,16,128,64]{2,3,1,0:T(8,128)} fusion(bf16[128,4,16,64]{0,3,2,1:T(8,128)(2,1)S(1)} %bitcast.86, f32[4,128,128]{2,1,0:T(8,128)S(1)} %fusion.44, f32[4,16,128]{2,1,0:T(8,128)} %bitcast.107, f32[4,16,128]{2,1,0:T(8,128)S(1)} %bitcast.109, pred[128,128]{1,0:T(8,128)(4,1)S(1)} %fusion.51), kind=kOutput, calls=%fused_computation.75 | convolution fusion | flops 140509184 | bytes 3489792 | tf_op jit(solution)/shard_map/ghts,sghp->tghp/dot_general | solution.py:53
  109.7 0.9 reshape.551
  110.6 1.6 copy.251
  114.3 1.6 copy.247
  115.9 8.0 %conditional.5 = (f32[4,8,128]{2,1,0:T(8,128)}, f32[4,8,128]{2,1,0:T(8,128)S(1)}, f32[4,8,128,128]{3,2,1,0:T(8,128)S(1)}) conditional(s32[]{:T(128)} %convert_element_type.137, () %tuple.41, (s32[128]{0:T(128)S(1)}, s32[32]{0:T(128)S(1)}, s32[]{:T(128)}, s32[128]{0:T(128)S(1)}, bf16[128,512]{1,0:T(8,128)(2,1)}, ...), branch_computations={%region_6.7_spmd, %region_7.11_spmd} | conditional | flops 272707712 | bytes 18830008 | solution.py:170
  116.1 0.9 reshape.530
  118.8 1.1 fusion.1
  120.7 0.9 reshape.531
  121.6 2.3 %convolution_add_fusion = f32[4,8,128,128]{3,2,1,0:T(8,128)S(1)} fusion(f32[4,8,128,128]{2,3,1,0:T(8,128)} %copy-done.5, f32[4,8,128]{2,1,0:T(8,128)S(1)} %get-tuple-element.477, f32[4,8,128]{2,1,0:T(8,128)} %get-tuple-element.513, bf16[128,4,128,1]{2,1,0,3:T(4,128)(2,1)S(1)} %bitcast.104), kind=kOutput, calls=%fused_computation.4 | convolution fusion | flops 135790592 | bytes 4358144 | tf_op jit(solution)/shard_map/cond/branch_1_fun/ngtk,knd->ngtd/dot_general | solution.py:104
  123.9 24.8 %collective-permute-done.4 = bf16[128,512]{1,0:T(8,128)(2,1)} collective-permute-done((bf16[128,512]{1,0:T(8,128)(2,1)}, bf16[128,512]{1,0:T(8,128)(2,1)}, u32[]{:S(2)}, u32[]{:S(2)}) %collective-permute-start.4) | collective-permute-done | bytes 131104 | tf_op jit(solution)/shard_map/ppermute | solution.py:20
  148.7 1.3 collective-permute-start.8
  150.0 1.5 collective-permute-done.5
  151.5 1.3 collective-permute-start.9
  152.8 1.3 collective-permute-start.10
  154.1 1.3 collective-permute-start.11
  155.4 8.1 %conditional.6 = ((f32[4,8,128]{2,1,0:T(8,128)}, f32[4,8,128]{2,1,0:T(8,128)S(1)}, f32[4,8,128,128]{3,2,1,0:T(8,128)S(1)})) conditional(s32[]{:T(128)} %convert_element_type.136, (f32[4,8,128]{2,1,0:T(8,128)}, f32[4,8,128]{2,1,0:T(8,128)S(1)}, f32[4,8,128,128]{3,2,1,0:T(8,128)S(1)}) %conditional.5, (s32[128]{0:T(128)S(1)}, s32[32]{0:T(128)S(1)}, ...), branch_computations={%region_11.12_spmd, %region_12.16_spmd} | conditional | flops 273223808 | bytes 21009088 | solution.py:170
  155.7 0.9 reshape.532
  157.1 0.7 max.8
  159.6 0.9 reshape.533
  160.5 2.4 %multiply_add_fusion = f32[4,8,128,128]{3,2,1,0:T(8,128)S(1)} fusion(f32[4,8,128,128]{3,2,1,0:T(8,128)S(1)} %get-tuple-element.131, f32[4,8,128,128]{2,3,1,0:T(8,128)} %copy-done.1, f32[4,8,128]{2,1,0:T(8,128)S(1)} %get-tuple-element.480, f32[4,8,128]{2,1,0:T(8,128)S(1)} %max.8, bf16[128,4,128,1]{2,1,0,3:T(4,128)(2,1)S(1)} %bitcast.98), kind=kOutput, calls=%fused_computation.16 | convolution fusion | flops 136314880 | bytes 6455296 | tf_op jit(solution)/shard_map/cond/branch_1_fun/ngtk,knd->ngtd/dot_general | solution.py:104
  163.5 8.0 %conditional.7 = ((f32[4,8,128]{2,1,0:T(8,128)}, f32[4,8,128]{2,1,0:T(8,128)S(1)}, f32[4,8,128,128]{3,2,1,0:T(8,128)S(1)})) conditional(s32[]{:T(128)} %convert_element_type.135, (f32[4,8,128]{2,1,0:T(8,128)}, f32[4,8,128]{2,1,0:T(8,128)S(1)}, f32[4,8,128,128]{3,2,1,0:T(8,128)S(1)}) %get-tuple-element.538, (s32[128]{0:T(128)S(1)}, ...), branch_computations={%region_16.17_spmd, %region_17.21_spmd} | conditional | flops 273223808 | bytes 21009088 | solution.py:170
  163.7 0.9 reshape.534
  165.1 0.7 max.9
  167.6 0.9 reshape.535
  168.5 2.4 %multiply_add_fusion.2 = f32[4,8,128,128]{3,2,1,0:T(8,128)S(1)} fusion(f32[4,8,128,128]{3,2,1,0:T(8,128)S(1)} %get-tuple-element.141, f32[4,8,128,128]{2,3,1,0:T(8,128)} %copy-done.2, f32[4,8,128]{2,1,0:T(8,128)S(1)} %get-tuple-element.482, f32[4,8,128]{2,1,0:T(8,128)S(1)} %max.9, bf16[128,4,128,1]{2,1,0,3:T(4,128)(2,1)S(1)} %bitcast.100), kind=kOutput, calls=%fused_computation.30 | convolution fusion | flops 136314880 | bytes 6455296 | tf_op jit(solution)/shard_map/cond/branch_1_fun/ngtk,knd->ngtd/dot_general | solution.py:104
  171.5 8.0 %conditional.8 = ((f32[4,8,128]{2,1,0:T(8,128)}, f32[4,8,128]{2,1,0:T(8,128)S(1)}, f32[4,8,128,128]{3,2,1,0:T(8,128)S(1)})) conditional(s32[]{:T(128)} %convert_element_type.134, (f32[4,8,128]{2,1,0:T(8,128)}, f32[4,8,128]{2,1,0:T(8,128)S(1)}, f32[4,8,128,128]{3,2,1,0:T(8,128)S(1)}) %get-tuple-element.539, (s32[128]{0:T(128)S(1)}, ...), branch_computations={%region_21.22_spmd, %region_22.26_spmd} | conditional | flops 273223808 | bytes 21009088 | solution.py:170
  171.8 0.9 reshape.536
  173.1 0.7 max.10
  175.6 0.9 reshape.537
  176.6 2.4 %multiply_add_fusion.4 = f32[4,8,128,128]{3,2,1,0:T(8,128)S(1)} fusion(f32[4,8,128,128]{3,2,1,0:T(8,128)S(1)} %get-tuple-element.151, f32[4,8,128,128]{2,3,1,0:T(8,128)} %copy-done.3, f32[4,8,128]{2,1,0:T(8,128)S(1)} %get-tuple-element.484, f32[4,8,128]{2,1,0:T(8,128)S(1)} %max.10, bf16[128,4,128,1]{2,1,0,3:T(4,128)(2,1)S(1)} %bitcast.102), kind=kOutput, calls=%fused_computation.44 | convolution fusion | flops 136314880 | bytes 6455296 | tf_op jit(solution)/shard_map/cond/branch_1_fun/ngtk,knd->ngtd/dot_general | solution.py:104
  179.6 6.5 %conditional.9 = ((f32[4,8,128]{2,1,0:T(8,128)S(1)}, f32[4,8,128,128]{3,2,1,0:T(8,128)S(1)})) conditional(s32[]{:T(128)} %convert_element_type.133, (f32[4,8,128]{2,1,0:T(8,128)S(1)}, f32[4,8,128,128]{3,2,1,0:T(8,128)S(1)}) %tuple.46, (s32[128]{0:T(128)S(1)}, s32[32]{0:T(128)S(1)}, s32[]{:T(128)}, s32[128]{0:T(128)S(1)}, ...), branch_computations={%region_26.27_spmd, %region_27.31_spmd} | conditional | flops 273223808 | bytes 20976312 | solution.py:170
  182.8 0.9 reshape.539
  183.7 2.4 %multiply_add_fusion.6 = f32[4,8,128,128]{3,2,1,0:T(8,128)S(1)} fusion(f32[4,8,128,128]{3,2,1,0:T(8,128)S(1)} %get-tuple-element.161, f32[4,8,128,128]{2,3,1,0:T(8,128)} %copy-done.4, f32[4,8,128]{2,1,0:T(8,128)S(1)} %get-tuple-element.486, f32[4,8,128]{2,1,0:T(8,128)S(1)} %max.11, bf16[128,4,128,1]{2,1,0,3:T(4,128)(2,1)S(1)} %bitcast.95), kind=kOutput, calls=%fused_computation.58 | convolution fusion | flops 136314880 | bytes 6455296 | tf_op jit(solution)/shard_map/cond/branch_1_fun/ngtk,knd->ngtd/dot_general | solution.py:104
  187.5 1.3 convert_element_type.140
  188.8 3.7 %all-to-all-start.1 = ((bf16[2,64,4096]{2,1,0:T(8,128)(2,1)}), bf16[2,64,4096]{2,1,0:T(8,128)(2,1)S(1)}, u32[]{:S(2)}, u32[]{:S(2)}) async-start(bf16[2,64,4096]{2,1,0:T(8,128)(2,1)} %convert_element_type.140), calls=%async_computation.1 | async-start | bytes 2097152 | tf_op jit(solution)/shard_map/all_to_all | solution.py:187
  192.6 6.6 %multiply_reduce_fusion = (f32[128,4]{0,1:T(4,128)S(1)}, f32[128,4,16,64]{0,3,2,1:T(8,128)}) fusion(f32[128,4,16,64]{0,3,2,1:T(8,128)S(1)} %bitcast.87, f32[128,4,16]{0,2,1:T(8,128)S(1)} %broadcast_multiply_fusion, f32[4,16,64,256]{3,2,1,0:T(8,128)} %collective-permute-done.3, bf16[128,4,256,1]{2,1,0,3:T(4,128)(2,1)S(1)} %bitcast.105, ...), kind=kOutput, calls=%fused_computation.81 | convolution fusion | flops 1615330816 | bytes 10782720 | tf_op jit(solution)/shard_map/tgn,ghpn->tghp/dot_general | solution.py:72
  199.6 1.6 copy.309
  201.3 2.9 %copy.249 = f32[128,4096]{1,0:T(8,128)} copy(f32[128,4096]{0,1:T(8,128)} %bitcast.88) | data formatting | bytes 4194304 | tf_op jit(solution)/shard_map/reshape | solution.py:75
  204.2 1.8 multiply_convert_fusion.2
  206.1 1.1 pad_maximum_fusion
  207.2 3.6 %all-to-all-start = ((bf16[2,64,4096]{2,1,0:T(8,128)(2,1)}), bf16[2,64,4096]{2,1,0:T(8,128)(2,1)S(1)}, u32[]{:S(2)}, u32[]{:S(2)}) async-start(bf16[2,64,4096]{2,1,0:T(8,128)(2,1)} %pad_maximum_fusion), calls=%async_computation | async-start | bytes 2097152 | tf_op jit(solution)/shard_map/all_to_all | solution.py:182
  210.8 1.0 copy.308
  211.8 8.3 %all-to-all-done = bf16[2,64,4096]{2,1,0:T(8,128)(2,1)S(1)} async-done(((bf16[2,64,4096]{2,1,0:T(8,128)(2,1)}), bf16[2,64,4096]{2,1,0:T(8,128)(2,1)S(1)}, u32[]{:S(2)}, u32[]{:S(2)}) %all-to-all-start) | async-done | bytes 1048608 | tf_op jit(solution)/shard_map/all_to_all | solution.py:182
  220.1 1.0 copy.307
  (102 shorter events, 20.6 us)
Async XLA Ops:
  0.6 9.4 %copy-start.8 = (bf16[128,1024]{1,0:T(8,128)(2,1)S(1)}, bf16[128,1024]{1,0:T(8,128)(2,1)}, u32[]{:S(2)}) copy-start(bf16[128,1024]{1,0:T(8,128)(2,1)} %param.24) | copy-start | bytes 786436
  2.9 4.5 %copy-start.12 = (s32[32]{0:T(128)}, s32[32]{0:T(128)S(1)}, u32[]{:S(2)}) copy-start(s32[32]{0:T(128)S(1)} %get-tuple-element.487) | copy-start | bytes 388
  13.6 27.6 %collective-permute-start.1 = (bf16[4,16,64,256]{3,2,1,0:T(8,128)(2,1)}, bf16[4,16,64,256]{3,2,1,0:T(8,128)(2,1)S(1)}, u32[]{:S(2)}, u32[]{:S(2)}) collective-permute-start(bf16[4,16,64,256]{3,2,1,0:T(8,128)(2,1)} %get-tuple-element.506), channel_id=1, source_target_pairs={{0,2},{2,4},{4,6},{6,8},{8,10},{10,12},{12,14},{14,16},{16,18},{18... | collective-permute-start | bytes 6291464 | tf_op jit(solution)/shard_map/ppermute | solution.py:20
  41.1 50.4 %copy-start = (f32[4,16,64,256]{3,2,1,0:T(8,128)S(1)}, f32[4,16,64,256]{3,2,1,0:T(8,128)}, u32[]{:S(2)}) copy-start(f32[4,16,64,256]{3,2,1,0:T(8,128)} %get-tuple-element.507) | copy-start | bytes 12582916
  44.0 47.5 %collective-permute-start.2 = (bf16[4,16,64,256]{3,2,1,0:T(8,128)(2,1)S(1)}, bf16[4,16,64,256]{3,2,1,0:T(8,128)(2,1)S(1)}, u32[]{:S(2)}, u32[]{:S(2)}) collective-permute-start(bf16[4,16,64,256]{3,2,1,0:T(8,128)(2,1)S(1)} %fusion.31), channel_id=1, source_target_pairs={{0,4},{2,6},{4,8},{6,10},{8,12},{10,14},{12,16},{14,18},{16,20},{1... | collective-permute-start | bytes 6291464 | tf_op jit(solution)/shard_map/ppermute | solution.py:20
  45.3 43.2 %collective-permute-start = (bf16[4,16]{1,0:T(4,128)(2,1)S(1)}, bf16[4,16]{1,0:T(4,128)(2,1)S(1)}, u32[]{:S(2)}, u32[]{:S(2)}) collective-permute-start(bf16[4,16]{1,0:T(4,128)(2,1)S(1)} %convert_element_type.120), channel_id=1, source_target_pairs={{0,2},{2,4},{4,6},{6,8},{8,10},{10,12},{12,14},{14,16},{16,18},{18... | collective-permute-start | bytes 392 | tf_op jit(solution)/shard_map/ppermute | solution.py:20
  94.4 98.2 %collective-permute-start.3 = (f32[4,16,64,256]{3,2,1,0:T(8,128)}, f32[4,16,64,256]{3,2,1,0:T(8,128)}, u32[]{:S(2)}, u32[]{:S(2)}) collective-permute-start(f32[4,16,64,256]{3,2,1,0:T(8,128)} %multiply_add_fusion.8), channel_id=1, source_target_pairs={{0,2},{2,4},{4,6},{6,8},{8,10},{10,12},{12,14},{14,16},{16,18},{18... | collective-permute-start | bytes 12582920 | tf_op jit(solution)/shard_map/ppermute | solution.py:20
  96.3 52.4 %collective-permute-start.4 = (bf16[128,512]{1,0:T(8,128)(2,1)}, bf16[128,512]{1,0:T(8,128)(2,1)}, u32[]{:S(2)}, u32[]{:S(2)}) collective-permute-start(bf16[128,512]{1,0:T(8,128)(2,1)} %param.30), channel_id=1, source_target_pairs={{0,2},{2,4},{4,6},{6,8},{8,10},{10,12},{12,14},{14,16},{16,18},{18... | collective-permute-start | bytes 393224 | tf_op jit(solution)/shard_map/ppermute | solution.py:20
  98.2 54.6 %collective-permute-start.6 = (bf16[128,512]{1,0:T(8,128)(2,1)}, bf16[128,512]{1,0:T(8,128)(2,1)}, u32[]{:S(2)}, u32[]{:S(2)}) collective-permute-start(bf16[128,512]{1,0:T(8,128)(2,1)} %param.30), channel_id=1, source_target_pairs={{0,4},{2,6},{4,8},{6,10},{8,12},{10,14},{12,16},{14,18},{16,20},{1... | collective-permute-start | bytes 393224 | tf_op jit(solution)/shard_map/ppermute | solution.py:20
  99.5 52.0 %collective-permute-start.5 = (bf16[128,512]{1,0:T(8,128)(2,1)}, bf16[128,512]{1,0:T(8,128)(2,1)}, u32[]{:S(2)}, u32[]{:S(2)}) collective-permute-start(bf16[128,512]{1,0:T(8,128)(2,1)} %param.31), channel_id=1, source_target_pairs={{0,2},{2,4},{4,6},{6,8},{8,10},{10,12},{12,14},{14,16},{16,18},{18... | collective-permute-start | bytes 393224 | tf_op jit(solution)/shard_map/ppermute | solution.py:20
  101.5 52.7 %collective-permute-start.7 = (bf16[128,512]{1,0:T(8,128)(2,1)}, bf16[128,512]{1,0:T(8,128)(2,1)}, u32[]{:S(2)}, u32[]{:S(2)}) collective-permute-start(bf16[128,512]{1,0:T(8,128)(2,1)} %param.31), channel_id=1, source_target_pairs={{0,4},{2,6},{4,8},{6,10},{8,12},{10,14},{12,16},{14,18},{16,20},{1... | collective-permute-start | bytes 393224 | tf_op jit(solution)/shard_map/ppermute | solution.py:20
  104.1 5.6 %copy-start.9 = (bf16[128,1024]{1,0:T(8,128)(2,1)S(1)}, bf16[128,1024]{1,0:T(8,128)(2,1)}, u32[]{:S(2)}) copy-start(bf16[128,1024]{1,0:T(8,128)(2,1)} %param.25) | copy-start | bytes 786436
  108.3 6.0 %copy-start.7 = (bf16[128,4096]{1,0:T(8,128)(2,1)S(1)}, bf16[128,4096]{1,0:T(8,128)(2,1)}, u32[]{:S(2)}) copy-start(bf16[128,4096]{1,0:T(8,128)(2,1)} %param.23) | copy-start | bytes 3145732
  108.3 6.0 %copy-start.13 = (s32[32]{0:T(128)S(1)}, s32[32]{0:T(128)}, u32[]{:S(2)}) copy-start(s32[32]{0:T(128)} %copy-done.12) | copy-start | bytes 388
  117.5 1.4 copy-start.5
  148.7 22.8 %collective-permute-start.8 = (bf16[128,512]{1,0:T(8,128)(2,1)}, bf16[128,512]{1,0:T(8,128)(2,1)}, u32[]{:S(2)}, u32[]{:S(2)}) collective-permute-start(bf16[128,512]{1,0:T(8,128)(2,1)} %param.30), channel_id=1, source_target_pairs={{0,6},{2,8},{4,10},{6,12},{8,14},{10,16},{12,18},{14,20},{16,22},{... | collective-permute-start | bytes 393224 | tf_op jit(solution)/shard_map/ppermute | solution.py:20
  151.5 20.0 %collective-permute-start.9 = (bf16[128,512]{1,0:T(8,128)(2,1)}, bf16[128,512]{1,0:T(8,128)(2,1)}, u32[]{:S(2)}, u32[]{:S(2)}) collective-permute-start(bf16[128,512]{1,0:T(8,128)(2,1)} %param.31), channel_id=1, source_target_pairs={{0,6},{2,8},{4,10},{6,12},{8,14},{10,16},{12,18},{14,20},{16,22},{... | collective-permute-start | bytes 393224 | tf_op jit(solution)/shard_map/ppermute | solution.py:20
  152.8 26.7 %collective-permute-start.10 = (bf16[128,512]{1,0:T(8,128)(2,1)}, bf16[128,512]{1,0:T(8,128)(2,1)S(1)}, u32[]{:S(2)}, u32[]{:S(2)}) collective-permute-start(bf16[128,512]{1,0:T(8,128)(2,1)} %param.30), channel_id=1, source_target_pairs={{0,8},{2,10},{4,12},{6,14},{8,16},{10,18},{12,20},{14,22},{16,24},... | collective-permute-start | bytes 393224 | tf_op jit(solution)/shard_map/ppermute | solution.py:20
  154.1 25.4 %collective-permute-start.11 = (bf16[128,512]{1,0:T(8,128)(2,1)}, bf16[128,512]{1,0:T(8,128)(2,1)}, u32[]{:S(2)}, u32[]{:S(2)}) collective-permute-start(bf16[128,512]{1,0:T(8,128)(2,1)} %param.31), channel_id=1, source_target_pairs={{0,8},{2,10},{4,12},{6,14},{8,16},{10,18},{12,20},{14,22},{16,24},... | collective-permute-start | bytes 393224 | tf_op jit(solution)/shard_map/ppermute | solution.py:20
  157.1 1.4 copy-start.1
  165.1 1.4 copy-start.2
  173.1 1.4 copy-start.3
  180.3 1.4 copy-start.4
  187.5 5.0 %copy-start.10 = (bf16[128,4,256]{2,1,0:T(4,128)(2,1)S(1)}, bf16[128,4,256]{2,1,0:T(4,128)(2,1)}, u32[]{:S(2)}) copy-start(bf16[128,4,256]{2,1,0:T(4,128)(2,1)} %reshape.551) | copy-start | bytes 786436
  188.8 3.7 %copy-start.6 = (f32[128,4096]{0,1:T(8,128)S(1)}, f32[128,4096]{0,1:T(8,128)}, u32[]{:S(2)}) copy-start(f32[128,4096]{0,1:T(8,128)} %copy.247) | copy-start | bytes 6291460
  188.8 18.4 %all-to-all-start.1 = ((bf16[2,64,4096]{2,1,0:T(8,128)(2,1)}), bf16[2,64,4096]{2,1,0:T(8,128)(2,1)S(1)}, u32[]{:S(2)}, u32[]{:S(2)}) async-start(bf16[2,64,4096]{2,1,0:T(8,128)(2,1)} %convert_element_type.140), calls=%async_computation.1 | async-start | bytes 2097152 | tf_op jit(solution)/shard_map/all_to_all | solution.py:187
  201.3 2.9 %copy-start.11 = (f32[4096]{0:T(1024)S(1)}, f32[4096]{0:T(1024)}, u32[]{:S(2)}) copy-start(f32[4096]{0:T(1024)} %param.28) | copy-start | bytes 49156
  207.2 13.0 %all-to-all-start = ((bf16[2,64,4096]{2,1,0:T(8,128)(2,1)}), bf16[2,64,4096]{2,1,0:T(8,128)(2,1)S(1)}, u32[]{:S(2)}, u32[]{:S(2)}) async-start(bf16[2,64,4096]{2,1,0:T(8,128)(2,1)} %pad_maximum_fusion), calls=%async_computation | async-start | bytes 2097152 | tf_op jit(solution)/shard_map/all_to_all | solution.py:182
